TPU v7x, 32 devices: a whole 2x2x4 slice. The times are simulated.
32 devices in a mesh: dp: 8 (over y, x, core), tensor: 4 (over z).
Axes of the slice: x: 2, y: 2, z: 4, core: 2. Of those that a mesh axis runs over, the one named last changes fastest.
Arguments:
- short_tokens: bfloat16 [16, 256, 768], P('dp'), may hold values from -6 to 6
- short_lengths: int32 [16], P('dp'), may hold values from 64 to 256, as said below
- long_tokens: bfloat16 [24, 512, 768], P('dp'), may hold values from -6 to 6
- long_lengths: int32 [24], P('dp'), may hold values from 257 to 512, as said below
- w_qkv: bfloat16 [3, 768, 768], P(None, None, 'tensor'), may hold values from -0.21875 to 0.21875
- b_qv: bfloat16 [2, 12, 64], P(None, 'tensor'), may hold values from -3 to 3
- w_out: bfloat16 [768, 768], P('tensor'), may hold values from -2.5 to 2.5
- res_biases: bfloat16 [2, 768], replicated, may hold values from -3 to 3
- ln_gains: bfloat16 [2, 768], replicated, may hold values from 0.099609375 to 1.8984375
- ln_shifts: bfloat16 [2, 768], replicated, may hold values from -3 to 3
- w_up: bfloat16 [768, 3072], P(None, 'tensor'), may hold values from -0.21875 to 0.21875
- b_up: bfloat16 [4, 768], P('tensor'), may hold values from -3 to 3
- w_down: bfloat16 [3072, 768], P('tensor'), may hold values from -0.109375 to 0.109375
- short_cotangent: bfloat16 [16, 256, 768], P('dp'), may hold values from -6 to 6
- long_cotangent: bfloat16 [24, 512, 768], P('dp'), may hold values from -6 to 6
Outputs:
- short_encoded: bfloat16 [16, 256, 768], P('dp')
- long_encoded: bfloat16 [24, 512, 768], P('dp')
- short_grad_tokens: float32 [16, 256, 768], P('dp')
- long_grad_tokens: float32 [24, 512, 768], P('dp')
- grad_qkv: float32 [3, 768, 768], P(None, 'dp', 'tensor')
- grad_qv_bias: float32 [2, 12, 64], P(None, 'tensor', 'dp')
- grad_out: float32 [768, 768], P('tensor', 'dp')
- grad_res_biases: float32 [2, 768], P(None, 'dp')
- grad_gains: float32 [2, 768], P(None, 'dp')
- grad_shifts: float32 [2, 768], P(None, 'dp')
- grad_up: float32 [768, 3072], P('dp', 'tensor')
- grad_up_bias: float32 [4, 768], P('tensor', 'dp')
- grad_down: float32 [3072, 768], P('tensor', 'dp')
Inputs may be any that keep to these rules, and one draw needn't show every extreme that they name: `short_lengths`: the first short pair has 256 valid tokens. `long_lengths`: the first long pair has 512 valid tokens.
All inputs are finite; a program needn't handle non-finite values.
Results may differ from a plain program's by a relative error of at most 0.013.
The roundings to bfloat16 on the way count: a program that leaves them out, or rounds other values in their place, can miss the bound.
Values sent between devices are 32-bit elements; how exact they have to be, the bound alone decides.
No kernel may reach another device: no remote copies, remote signals or barrier semaphores. Data moves between devices by JAX's collectives and lax.ppermute only.
A program may use at most 128 MiB of HBM per device.

v0:
```python
import jax
import jax.numpy as jnp
from jax import lax
from jax.sharding import PartitionSpec as P

HD = 64
EPSILON = 1e-12


def normalize(hidden):
    center = hidden - jnp.mean(hidden, -1, keepdims=True)
    factor = lax.rsqrt(jnp.mean(center * center, -1, keepdims=True) + EPSILON)
    return (center * factor, factor[:, 0])


def norm_back(upstream, normed, factor, gain):
    scaled = upstream * gain
    inner_mean = jnp.mean(scaled, -1, keepdims=True)
    cross_mean = jnp.mean(scaled * normed, -1, keepdims=True)
    return factor[:, None] * (scaled - inner_mean - normed * cross_mean)


def gelu_exact(inner):
    return jax.nn.gelu(inner, approximate=False)


def masked_scores(queries, key_rows, length):
    scores = jnp.einsum(
        "qhe,khe->hqk", queries, key_rows, preferred_element_type=jnp.float32
    ) * HD ** (-0.5)
    visible = jnp.arange(key_rows.shape[0]) < length
    return jnp.where(visible[None, None, :], scores, -1e30)


def attend(queries, key_rows, value_rows, length):
    scores = masked_scores(queries, key_rows, length)
    largest = jnp.max(scores, -1, keepdims=True)
    weights_exp = jnp.exp(scores - largest)
    total = jnp.sum(weights_exp, -1, keepdims=True)
    probs = weights_exp / total
    mixed = jnp.einsum(
        "hqk,khe->qhe", probs.astype(jnp.bfloat16), value_rows, preferred_element_type=jnp.float32
    )
    log_total = largest[..., 0] + jnp.log(total[..., 0])
    return (mixed.astype(jnp.bfloat16), log_total)


def attend_back(queries, key_rows, value_rows, length, log_total, grad_mixed):
    scores = masked_scores(queries, key_rows, length)
    probs = jnp.exp(scores - log_total[..., None])
    grad_values = jnp.einsum(
        "hqk,qhe->khe", probs.astype(jnp.bfloat16), grad_mixed, preferred_element_type=jnp.float32
    )
    grad_probs = jnp.einsum(
        "qhe,khe->hqk", grad_mixed, value_rows, preferred_element_type=jnp.float32
    )
    centered = jnp.sum(probs * grad_probs, -1, keepdims=True)
    grad_scores = (probs * (grad_probs - centered)).astype(jnp.bfloat16)
    grad_queries = jnp.einsum(
        "hqk,khe->qhe", grad_scores, key_rows, preferred_element_type=jnp.float32
    ) * HD ** (-0.5)
    grad_keys = jnp.einsum(
        "hqk,qhe->khe", grad_scores, queries, preferred_element_type=jnp.float32
    ) * HD ** (-0.5)
    return (grad_queries, grad_keys, grad_values)


def forward_pair(item_tuple):
    pair_q, pair_k, pair_v, length = item_tuple
    return attend(pair_q, pair_k, pair_v, length)


def backward_pair(item_tuple):
    pair_q, pair_k, pair_v, length, pair_lse, pair_grad = item_tuple
    return attend_back(pair_q, pair_k, pair_v, length, pair_lse, pair_grad)


def on_device(
    short_tokens,
    short_lengths,
    long_tokens,
    long_lengths,
    w_qkv,
    b_qv,
    w_out,
    res_biases,
    ln_gains,
    ln_shifts,
    w_up,
    b_up,
    w_down,
    short_cotangent,
    long_cotangent,
):
    short_pairs, short_slot, model_width = short_tokens.shape
    long_pairs, long_slot = (long_tokens.shape[0], long_tokens.shape[1])
    short_rows = short_pairs * short_slot
    long_rows = long_pairs * long_slot
    local_width = w_qkv.shape[2]
    heads_here = b_qv.shape[1]
    head_size = b_qv.shape[2]
    flat = jnp.concatenate(
        [
            short_tokens.reshape(short_rows, model_width),
            long_tokens.reshape(long_rows, model_width),
        ],
        0,
    )
    flat_float = flat.astype(jnp.float32)
    gain_rows = ln_gains.astype(jnp.float32)
    shift_rows = ln_shifts.astype(jnp.float32)
    bias_float = res_biases.astype(jnp.float32)
    projected = jnp.einsum("rd,cde->cre", flat, w_qkv, preferred_element_type=jnp.float32)
    bias_rows = jnp.stack(
        [
            b_qv[0].reshape(local_width).astype(jnp.float32),
            jnp.zeros((local_width,), jnp.float32),
            b_qv[1].reshape(local_width).astype(jnp.float32),
        ]
    )
    projected = (projected + bias_rows[:, None, :]).astype(jnp.bfloat16)
    short_proj = projected[:, :short_rows].reshape(
        3, short_pairs, short_slot, heads_here, head_size
    )
    long_proj = projected[:, short_rows:].reshape(3, long_pairs, long_slot, heads_here, head_size)
    short_att, short_lse = lax.map(
        forward_pair, (short_proj[0], short_proj[1], short_proj[2], short_lengths)
    )
    long_att, long_lse = lax.map(
        forward_pair, (long_proj[0], long_proj[1], long_proj[2], long_lengths)
    )
    mixed = jnp.concatenate(
        [short_att.reshape(short_rows, local_width), long_att.reshape(long_rows, local_width)], 0
    )
    attn_part = jnp.dot(mixed, w_out, preferred_element_type=jnp.float32)
    attn_total = lax.psum(attn_part, "tensor")
    normed_one, factor_one = normalize(flat_float + attn_total + bias_float[0])
    first_out = normed_one * gain_rows[0] + shift_rows[0]
    first_low = first_out.astype(jnp.bfloat16)
    inner = jnp.dot(first_low, w_up, preferred_element_type=jnp.float32) + b_up[0].astype(
        jnp.float32
    )
    activated = gelu_exact(inner).astype(jnp.bfloat16)
    ffn_part = jnp.dot(activated, w_down, preferred_element_type=jnp.float32)
    ffn_total = lax.psum(ffn_part, "tensor")
    normed_two, factor_two = normalize(first_out + ffn_total + bias_float[1])
    encoded = (normed_two * gain_rows[1] + shift_rows[1]).astype(jnp.bfloat16)
    upstream = jnp.concatenate(
        [
            short_cotangent.reshape(short_rows, model_width),
            long_cotangent.reshape(long_rows, model_width),
        ],
        0,
    ).astype(jnp.float32)
    grad_second = norm_back(upstream, normed_two, factor_two, gain_rows[1])
    small_second = jnp.stack(
        [jnp.sum(grad_second, 0), jnp.sum(upstream * normed_two, 0), jnp.sum(upstream, 0)]
    )
    grad_branch = grad_second.astype(jnp.bfloat16)
    grad_down = jnp.einsum("rf,rd->fd", activated, grad_branch, preferred_element_type=jnp.float32)
    grad_activated = jnp.einsum(
        "rd,fd->rf", grad_branch, w_down, preferred_element_type=jnp.float32
    )
    ignored_value, gelu_pullback = jax.vjp(gelu_exact, inner)
    grad_inner = gelu_pullback(grad_activated)[0].astype(jnp.bfloat16)
    grad_up = jnp.einsum("rd,rf->df", first_low, grad_inner, preferred_element_type=jnp.float32)
    grad_up_bias = jnp.sum(grad_inner.astype(jnp.float32), 0)[None, :]
    input_part = jnp.einsum("rf,df->rd", grad_inner, w_up, preferred_element_type=jnp.float32)
    up_shard, down_shard, up_bias_shard, small_second_shard = (
        lax.psum_scatter(grad_up, "dp", scatter_dimension=0, tiled=True),
        lax.psum_scatter(grad_down, "dp", scatter_dimension=1, tiled=True),
        lax.psum_scatter(grad_up_bias, "dp", scatter_dimension=1, tiled=True),
        lax.psum_scatter(small_second, "dp", scatter_dimension=1, tiled=True),
    )
    grad_first_out = grad_second + lax.psum(input_part, "tensor")
    grad_first = norm_back(grad_first_out, normed_one, factor_one, gain_rows[0])
    small_first = jnp.stack(
        [
            jnp.sum(grad_first, 0),
            jnp.sum(grad_first_out * normed_one, 0),
            jnp.sum(grad_first_out, 0),
        ]
    )
    grad_attn = grad_first.astype(jnp.bfloat16)
    grad_out = jnp.einsum("rl,rd->ld", mixed, grad_attn, preferred_element_type=jnp.float32)
    grad_mixed = jnp.einsum(
        "rd,ld->rl", grad_attn, w_out, preferred_element_type=jnp.float32
    ).astype(jnp.bfloat16)
    short_grad_mixed = grad_mixed[:short_rows].reshape(
        short_pairs, short_slot, heads_here, head_size
    )
    long_grad_mixed = grad_mixed[short_rows:].reshape(long_pairs, long_slot, heads_here, head_size)
    short_gq, short_gk, short_gv = lax.map(
        backward_pair,
        (short_proj[0], short_proj[1], short_proj[2], short_lengths, short_lse, short_grad_mixed),
    )
    long_gq, long_gk, long_gv = lax.map(
        backward_pair,
        (long_proj[0], long_proj[1], long_proj[2], long_lengths, long_lse, long_grad_mixed),
    )
    short_grads = (
        jnp.stack([short_gq, short_gk, short_gv])
        .astype(jnp.bfloat16)
        .reshape(3, short_rows, local_width)
    )
    long_grads = (
        jnp.stack([long_gq, long_gk, long_gv])
        .astype(jnp.bfloat16)
        .reshape(3, long_rows, local_width)
    )
    grad_projected = jnp.concatenate([short_grads, long_grads], 1)
    grad_qkv = jnp.einsum("rd,cre->cde", flat, grad_projected, preferred_element_type=jnp.float32)
    grad_bias_rows = jnp.sum(grad_projected.astype(jnp.float32), 1)
    grad_qv_bias = jnp.stack([grad_bias_rows[0], grad_bias_rows[2]]).reshape(
        2, heads_here, head_size
    )
    token_part = jnp.einsum(
        "cre,cde->rd", grad_projected, w_qkv, preferred_element_type=jnp.float32
    )
    qkv_shard, qv_bias_shard, out_shard, small_first_shard = (
        lax.psum_scatter(grad_qkv, "dp", scatter_dimension=1, tiled=True),
        lax.psum_scatter(grad_qv_bias, "dp", scatter_dimension=2, tiled=True),
        lax.psum_scatter(grad_out, "dp", scatter_dimension=1, tiled=True),
        lax.psum_scatter(small_first, "dp", scatter_dimension=1, tiled=True),
    )
    grad_tokens = grad_first + lax.psum(token_part, "tensor")
    grad_res_biases = jnp.concatenate([small_first_shard[0:1], small_second_shard[0:1]], 0)
    grad_gains = jnp.concatenate([small_first_shard[1:2], small_second_shard[1:2]], 0)
    grad_shifts = jnp.concatenate([small_first_shard[2:3], small_second_shard[2:3]], 0)
    return (
        encoded[:short_rows].reshape(short_pairs, short_slot, model_width),
        encoded[short_rows:].reshape(long_pairs, long_slot, model_width),
        grad_tokens[:short_rows].reshape(short_pairs, short_slot, model_width),
        grad_tokens[short_rows:].reshape(long_pairs, long_slot, model_width),
        qkv_shard,
        qv_bias_shard,
        out_shard,
        grad_res_biases,
        grad_gains,
        grad_shifts,
        up_shard,
        up_bias_shard,
        down_shard,
    )


def solution(mesh):
    return jax.shard_map(
        on_device,
        mesh=mesh,
        in_specs=(
            P("dp", None, None),
            P("dp"),
            P("dp", None, None),
            P("dp"),
            P(None, None, "tensor"),
            P(None, "tensor", None),
            P("tensor", None),
            P(),
            P(),
            P(),
            P(None, "tensor"),
            P("tensor", None),
            P("tensor", None),
            P("dp", None, None),
            P("dp", None, None),
        ),
        out_specs=(
            P("dp", None, None),
            P("dp", None, None),
            P("dp", None, None),
            P("dp", None, None),
            P(None, "dp", "tensor"),
            P(None, "tensor", "dp"),
            P("tensor", "dp"),
            P(None, "dp"),
            P(None, "dp"),
            P(None, "dp"),
            P("dp", "tensor"),
            P("tensor", "dp"),
            P("tensor", "dp"),
        ),
        check_vma=False,
    )
```

profile of v0, /device:TPU:0, one launch (start us, length us, event | category | flops | bytes accessed | tf_op | source)
XLA Modules:
  0.0 1305.4 jit_solution(6530653363544916583)
XLA Ops:
  8.3 4.1 fusion.122
  15.2 2.1 squeeze.91
  17.3 1.3 copy.102
  19.7 1.3 copy.103
  21.0 15.0 %while.53 = (s32[]{:T(128)}, bf16[3,512,3,64]{1,3,2,0:T(8,128)(2,1)}, f32[3,3,512]{2,1,0:T(4,128)}, bf16[3,512,3,64]{1,3,2,0:T(8,128)(2,1)S(1)}, s32[3]{0:T(128)...) while((s32[]{:T(128)}, bf16[3,512,3,64]{1,3,2,0:T(8,128)(2,1)}, ...), condition=%wide.region_7.8_spmd, body=%wide.region_4.7_spmd.sunk | while | flops 210861056 | bytes 10283621 | solution.py:129
  24.4 1.6 fusion.200
  29.4 1.6 fusion.200
  34.4 1.6 fusion.200
  36.0 1.8 copy.104
  38.9 1.7 squeeze.88
  43.2 5.3 while.52
  48.5 1.2 copy.100
  50.9 4.7 fusion.137
  58.1 223.2 %all-reduce.6.cloned.1.call-done = f32[2048,768]{1,0:T(8,128)} async-done(((f32[2048,768]{1,0:T(8,128)}), f32[2048,768]{1,0:T(8,128)}) %all-reduce.6.cloned.1.call-update) | async-done | bytes 6291472 | tf_op jit(solution)/shard_map/psum | solution.py:136
  281.3 4.2 fusion.130
  288.2 18.4 %multiply_convert_fusion.2 = (bf16[2048,768]{1,0:T(8,128)(2,1)S(1)}, f32[2048,768]{1,0:T(8,128)}, f32[2048,768]{1,0:T(8,128)}) fusion(f32[768]{0:T(1024)S(1)} %copy-done.32, bf16[2048,768]{1,0:T(8,128)(2,1)S(1)} %fusion.103, bf16[768,768]{1,0:T(8,128)(2,1)S(1)} %copy-done), kind=kOutput, calls=%fused_computation.132 | convolution fusion | flops 2519728128 | bytes 20057088 | tf_op jit(solution)/shard_map/dot_general | solution.py:140
  306.6 1.7 copy-done.46
  308.3 4.6 fusion.138
  313.1 221.7 %all-reduce.8.cloned.1.call-done = f32[2048,768]{1,0:T(8,128)} async-done(((f32[2048,768]{1,0:T(8,128)}), f32[2048,768]{1,0:T(8,128)}) %all-reduce.8.cloned.1.call-update) | async-done | bytes 6291472 | tf_op jit(solution)/shard_map/psum | solution.py:145
  534.8 5.7 fusion.128
  542.4 4.6 fusion.97
  547.0 5.8 fusion.126
  552.9 9.5 convert_reduce_fusion.1
  562.4 1.8 copy-done.45
  564.2 4.5 fusion.139
  571.6 219.0 %all-reduce.10.cloned.1.call-done = f32[2048,768]{1,0:T(8,128)} async-done(((f32[2048,768]{1,0:T(8,128)}), f32[2048,768]{1,0:T(8,128)}) %all-reduce.10.cloned.1.call-update) | async-done | bytes 6291472 | tf_op jit(solution)/shard_map/psum | solution.py:175
  790.6 8.1 multiply_reduce_fusion.2
  798.8 4.7 fusion.125
  803.5 2.6 copy-done.3
  806.2 1.2 convolution_convert_fusion.1
  808.4 2.1 reshape.231
  810.5 1.3 copy.114
  811.8 25.9 %while.55 = (s32[]{:T(128)}, bf16[3,512,3,64]{1,3,2,0:T(8,128)(2,1)}, bf16[3,512,3,64]{1,3,2,0:T(8,128)(2,1)}, bf16[3,512,3,64]{1,3,2,0:T(8,128)(2,1)}, bf16[3,5...) while((s32[]{:T(128)}, ...), condition=%wide.region_24.25_spmd, body=%wide.region_22.24_spmd.sunk | while | flops 510589952 | bytes 35625200 | solution.py:197
  811.8 1.5 fusion.221
  819.2 1.3 fusion.224
  820.4 1.5 fusion.221
  827.8 1.3 fusion.224
  829.0 1.5 fusion.221
  836.4 1.3 fusion.224
  838.7 5.1 fusion.119
  844.2 9.6 while.54
  853.9 1.2 copy.109
  859.1 1.6 copy.116
  861.5 1.6 copy.117
  863.9 1.6 copy.118
  866.3 5.1 fusion.116
  871.4 4.3 copy.129
  875.7 4.7 reshape.242
  880.5 6.0 convolution_bitcast_fusion.1
  886.5 7.9 fusion.110
  894.8 7.0 fusion.140
  903.1 3.2 slice.147
  906.3 2.1 slice.146
  908.4 1.4 copy.140
  912.1 13.6 %all-reduce = f32[2,3,64]{2,1,0:T(4,128)S(1)} all-reduce(f32[2,3,64]{2,1,0:T(4,128)S(1)} %reshape.234), channel_id=3, replica_groups=mesh['dp'=8,'tensor'=4] {'dp'}, use_global_device_ids=true, to_apply=%region_28.29.clone | all-reduce | flops 384 | bytes 3072
  929.4 8.8 reduce-scatter.25.cloned.1.call-done
  938.2 1.6 copy.134
  939.8 42.0 %reduce-scatter.23.cloned.1.call-done = f32[96,576]{1,0:T(8,128)} async-done(((f32[768,576]{1,0:T(8,128)}), f32[96,576]{1,0:T(8,128)}) %reduce-scatter.23.cloned.1.call-update) | async-done | bytes 221200
  983.6 223.4 %all-reduce.12.cloned.1.call-done = f32[2048,768]{1,0:T(8,128)} async-done(((f32[2048,768]{1,0:T(8,128)}), f32[2048,768]{1,0:T(8,128)}) %all-reduce.12.cloned.1.call-update) | async-done | bytes 6291472 | tf_op jit(solution)/shard_map/psum | solution.py:226
  1207.0 5.5 add.175
  1212.5 2.5 slice.151
  1215.0 1.2 slice.150
  1216.2 35.8 %reduce-scatter.21.cloned.1.call-done = f32[768,96]{0,1:T(8,128)} async-done(((f32[768,768]{0,1:T(8,128)}), f32[768,96]{0,1:T(8,128)}) %reduce-scatter.21.cloned.1.call-update) | async-done | bytes 294928 | tf_op jit(solution)/shard_map/reduce_scatter | solution.py:171
  1252.0 46.3 %reduce-scatter.19.cloned.1.call-done = f32[96,768]{1,0:T(8,128)} async-done(((f32[768,768]{1,0:T(8,128)}), f32[96,768]{1,0:T(8,128)}) %reduce-scatter.19.cloned.1.call-update) | async-done | bytes 294928 | tf_op jit(solution)/shard_map/reduce_scatter | solution.py:170
  (294 shorter events, 79.7 us)
Async XLA Ops:
  7.2 281.0 %copy-start = (bf16[768,768]{1,0:T(8,128)(2,1)S(1)}, bf16[768,768]{1,0:T(8,128)(2,1)}, u32[]{:S(2)}) copy-start(bf16[768,768]{1,0:T(8,128)(2,1)} %param.33) | copy-start | bytes 3538948
  7.2 274.1 %all-reduce.6.cloned.1.call-start = ((), (), s32[]{:S(2)}) async-start(), calls=%async_computation.7 | async-start | bytes 12582912 | tf_op jit(solution)/shard_map/psum | solution.py:136
  12.8 8.1 copy-start.40
  21.0 20.5 %copy-start.16 = (bf16[1,512,192]{1,2,0:T(8,128)(2,1)S(1)}, bf16[1,512,192]{1,2,0:T(8,128)(2,1)}, u32[]{:S(2)}) copy-start(bf16[1,512,192]{1,2,0:T(8,128)(2,1)} %get-tuple-element.455) | copy-start | bytes 589828
  21.0 22.1 %copy-start.42 = (s32[2]{0:T(128)S(1)}, s32[2]{0:T(128)}, u32[]{:S(2)}) copy-start(s32[2]{0:T(128)} %param.24) | copy-start | bytes 28
  36.0 7.1 copy-start.6
  48.5 1.2 copy-start.10
  48.5 7.1 copy-start.23
  50.9 5.3 copy-start.35
  50.9 5.4 copy-start.34
  55.6 479.2 %all-reduce.8.cloned.1.call-start = ((), (), s32[]{:S(2)}) async-start(), calls=%async_computation.8 | async-start | bytes 12582912 | tf_op jit(solution)/shard_map/psum | solution.py:145
  285.5 2.7 copy-start.2
  285.5 0.9 copy-start.21
  285.5 0.9 copy-start.26
  286.4 1.8 copy-start.32
  288.2 18.5 %copy-start.9 = (bf16[2048,768]{1,0:T(8,128)(2,1)}, bf16[2048,768]{1,0:T(8,128)(2,1)S(1)}, u32[]{:S(2)}) copy-start(bf16[2048,768]{1,0:T(8,128)(2,1)S(1)} %fusion.103) | copy-start | bytes 9437188
  288.2 20.2 %copy-start.38 = (bf16[768,768]{1,0:T(8,128)(2,1)S(1)}, bf16[768,768]{1,0:T(8,128)(2,1)}, u32[]{:S(2)}) copy-start(bf16[768,768]{1,0:T(8,128)(2,1)} %param.35) | copy-start | bytes 3538948
  306.6 1.7 copy-start.46
  312.9 477.7 %all-reduce.10.cloned.1.call-start = ((), (), s32[]{:S(2)}) async-start(), calls=%async_computation.9 | async-start | bytes 12582912 | tf_op jit(solution)/shard_map/psum | solution.py:175
  540.5 1.7 copy-start.5
  540.6 1.8 copy-start.7
  540.6 1.8 copy-start.25
  541.4 5.5 copy-start.29
  542.4 10.5 slice-start.1
  547.0 5.9 copy-start.33
  547.0 5.9 copy-start.39
  547.0 5.9 slice-start.2
  552.9 9.5 copy-start.4
  562.4 1.8 copy-start.45
  568.7 0.7 copy-start.31
  568.7 221.9 %copy-start.22 = (f32[768]{0:T(1024)S(1)}, f32[768]{0:T(1024)}, u32[]{:S(2)}) copy-start(f32[768]{0:T(1024)} %get-tuple-element.469) | copy-start | bytes 9220
  568.7 339.6 %reduce-scatter.31.cloned.1.call-start = ((), (), s32[]{:S(2)}) async-start(), calls=%async_computation.17 | async-start | bytes 442368
  570.3 339.4 %reduce-scatter.29.cloned.1.call-start = ((), (), s32[]{:S(2)}) async-start(), calls=%async_computation.16 | async-start | bytes 442368
  571.4 355.0 %reduce-scatter.27.cloned.1.call-start = ((), (), s32[]{:S(2)}) async-start(), calls=%async_computation.15 | async-start | bytes 442368
  798.8 7.4 copy-start.12
  803.5 2.7 copy-start.3
  803.5 8.3 copy-start.41
  807.3 1.1 copy-start.8
  815.3 2.0 copy-start.19
  816.5 1.5 copy-start.17
  817.9 1.2 copy-start.20
  818.3 0.8 copy-start.18
  823.9 2.0 copy-start.19
  825.1 1.5 copy-start.17
  826.5 1.2 copy-start.20
  826.9 0.8 copy-start.18
  832.5 2.0 copy-start.19
  833.7 1.5 copy-start.17
  835.2 1.2 copy-start.20
  835.6 0.8 copy-start.18
  837.7 6.1 slice-start
  837.7 6.6 copy-start.11
  837.7 6.6 copy-start.24
  837.7 6.6 copy-start.43
  838.7 99.5 %reduce-scatter.25.cloned.1.call-start = ((), (), s32[]{:S(2)}) async-start(), calls=%async_computation.14 | async-start | bytes 884736
  843.9 137.8 %reduce-scatter.23.cloned.1.call-start = ((), (), s32[]{:S(2)}) async-start(), calls=%async_computation.13 | async-start | bytes 2211840
  853.8 12.5 copy-start.13
  871.4 9.0 copy-start.14
  871.4 9.0 copy-start.15
  880.4 326.6 %all-reduce.12.cloned.1.call-start = ((), (), s32[]{:S(2)}) async-start(), calls=%async_computation.10 | async-start | bytes 12582912 | tf_op jit(solution)/shard_map/psum | solution.py:226
  886.5 365.6 %reduce-scatter.21.cloned.1.call-start = ((), (), s32[]{:S(2)}) async-start(), calls=%async_computation.12 | async-start | bytes 2654208 | tf_op jit(solution)/shard_map/reduce_scatter | solution.py:171
  894.5 7.3 copy-start.44
  894.5 403.9 %reduce-scatter.19.cloned.1.call-start = ((), (), s32[]{:S(2)}) async-start(), calls=%async_computation.11 | async-start | bytes 2654208 | tf_op jit(solution)/shard_map/reduce_scatter | solution.py:170
  1207.0 91.4 %copy-start.1 = (bf16[768,768]{1,0:T(8,128)(2,1)S(1)}, bf16[768,768]{1,0:T(8,128)(2,1)}, u32[]{:S(2)}) copy-start(bf16[768,768]{1,0:T(8,128)(2,1)} %param.33) | copy-start | bytes 3538948
  (5 other events, 3.4 us)
Sparse Core Ops, SparseCore 0:
  55.7 225.5 all-reduce.5
  313.0 221.7 all-reduce.7
  568.9 221.7 all-reduce.9
  793.5 32.7 reduce-scatter.30
  829.3 33.8 reduce-scatter.28
  866.1 33.8 reduce-scatter.26
  903.2 34.9 reduce-scatter.24
  941.6 40.1 reduce-scatter.22
  984.1 222.8 all-reduce.11
  1210.8 41.2 reduce-scatter.20
  1256.0 42.3 reduce-scatter.18
where the time goes:
time: 1310 us
  waiting for transfers between devices  1020 us (78%)
  matrix products  109 us (8%)
  local copies, waits for them, and re-layouts  84.2 us (6%)
  other arithmetic  59.6 us (5%)
  between operations  15.9 us (1%)
  blocking collectives  13.6 us (1%)
    psum x1, waiting for transfers between devices, on_device(): grad_tokens = grad_first + lax.psum(token_part, 'tensor')  223 us
    psum x1, waiting for transfers between devices, on_device(): attn_total = lax.psum(attn_part, 'tensor')  223 us
    psum x1, waiting for transfers between devices, on_device(): ffn_total = lax.psum(ffn_part, 'tensor')  222 us
    psum x1, waiting for transfers between devices, on_device(): grad_first_out = grad_second + lax.psum(input_part, 'tensor')  219 us
    unnamed x16, waiting for transfers between devices  50.9 us
    reduce_scatter x1, waiting for transfers between devices, on_device(): lax.psum_scatter(grad_up, 'dp', scatter_dimension=0, tiled=True)  46.3 us
    reduce_scatter x1, waiting for transfers between devices, on_device(): lax.psum_scatter(grad_down, 'dp', scatter_dimension=1, tiled=True)  35.8 us
    unnamed x111, local copies, waits for them, and re-layouts  27.9 us
  transfers between devices with their start and end apart: 11, of which 8 were waited for; matrix products, arithmetic and copies ran while one was open for 10% of the time, Pallas kernels for 0%

commit v1 on v0

--- a/solution.py
+++ b/solution.py
@@ -142,7 +142,7 @@
     )
     activated = gelu_exact(inner).astype(jnp.bfloat16)
     ffn_part = jnp.dot(activated, w_down, preferred_element_type=jnp.float32)
-    ffn_total = lax.psum(ffn_part, "tensor")
+    ffn_total = jnp.sum(lax.all_gather(ffn_part, "tensor"), axis=0)
     normed_two, factor_two = normalize(first_out + ffn_total + bias_float[1])
     encoded = (normed_two * gain_rows[1] + shift_rows[1]).astype(jnp.bfloat16)
     upstream = jnp.concatenate(

time: 1310 us -> 1520 us (1.16)
  waiting for transfers between devices: 1020 us -> 1230 us
    all_gather x0 -> x1, waiting for transfers between devices: none -> 424 us  [on_device(): ffn_total = jnp.sum(lax.all_gather(ffn_part, 'tensor'), axis=0)]
    psum x1 -> x0, waiting for transfers between devices: 222 us -> none  [on_device(): ffn_total = lax.psum(ffn_part, 'tensor')]
  transfers between devices with their start and end apart: 11 -> 11, of which waited for: 8 -> 8; matrix products, arithmetic and copies ran while one was open for 10% -> 8% of each run, Pallas kernels for 0% -> 0%
where the time goes in v1:
time: 1520 us; the launch traced here: 1510 us
  waiting for transfers between devices  1230 us (81%)
  matrix products  106 us (7%)
  local copies, waits for them, and re-layouts  75.9 us (5%)
  other arithmetic  68.6 us (5%)
  between operations  16.1 us (1%)
    all_gather x1, waiting for transfers between devices, on_device(): ffn_total = jnp.sum(lax.all_gather(ffn_part, 'tensor'), axis=0)  424 us
    psum x1, waiting for transfers between devices, on_device(): attn_total = lax.psum(attn_part, 'tensor')  225 us
    psum x1, waiting for transfers between devices, on_device(): grad_tokens = grad_first + lax.psum(token_part, 'tensor')  223 us
    psum x1, waiting for transfers between devices, on_device(): grad_first_out = grad_second + lax.psum(input_part, 'tensor')  219 us
    unnamed x16, waiting for transfers between devices  57 us
    reduce_scatter x1, waiting for transfers between devices, on_device(): lax.psum_scatter(grad_down, 'dp', scatter_dimension=1, tiled=True)  46.3 us
    reduce_scatter x1, waiting for transfers between devices, on_device(): lax.psum_scatter(grad_up, 'dp', scatter_dimension=0, tiled=True)  35.8 us
  transfers between devices with their start and end apart: 11, of which 8 were waited for; matrix products, arithmetic and copies ran while one was open for 8% of the time, Pallas kernels for 0%

profile of v1, /device:TPU:0, one launch (start us, length us, event | category | flops | bytes accessed | tf_op | source)
XLA Modules:
  0.0 1512.4 jit_solution(10701474615497624901)
XLA Ops:
  8.3 4.1 fusion.122
  12.9 1.2 fusion.132
  14.4 4.0 while.52
  19.1 1.4 squeeze.90
  21.5 2.1 squeeze.91
  23.6 1.3 copy.102
  24.9 2.1 squeeze.92
  27.0 1.3 copy.103
  28.3 16.0 %while.53 = (s32[]{:T(128)}, bf16[3,512,3,64]{1,3,2,0:T(8,128)(2,1)}, f32[3,3,512]{2,1,0:T(4,128)S(1)}, bf16[3,512,3,64]{1,3,2,0:T(8,128)(2,1)}, s32[3]{0:T(128)...) while((s32[]{:T(128)}, bf16[3,512,3,64]{1,3,2,0:T(8,128)(2,1)}, ...), condition=%wide.region_7.8_spmd, body=%wide.region_4.7_spmd.sunk | while | flops 210861056 | bytes 10283121 | solution.py:129
  31.0 2.6 fusion.200
  36.4 2.6 fusion.200
  41.7 2.6 fusion.200
  44.3 1.6 copy.104
  46.2 3.7 fusion.137
  50.6 225.0 %all-reduce.5.cloned.1.call-done = f32[2048,768]{1,0:T(8,128)} async-done(((f32[2048,768]{1,0:T(8,128)}), f32[2048,768]{1,0:T(8,128)}) %all-reduce.5.cloned.1.call-update) | async-done | bytes 6291472 | tf_op jit(solution)/shard_map/psum | solution.py:136
  275.6 4.2 fusion.130
  282.5 18.4 %multiply_convert_fusion.2 = (bf16[2048,768]{1,0:T(8,128)(2,1)S(1)}, f32[2048,768]{1,0:T(8,128)}, f32[2048,768]{1,0:T(8,128)}) fusion(f32[768]{0:T(1024)S(1)} %convert_reduce_fusion.3, bf16[2048,768]{1,0:T(8,128)(2,1)S(1)} %fusion.103, bf16[768,768]{1,0:T(8,128)(2,1)S(1)} %copy-done), kind=kOutput, calls=%fused_computation.132 | convolution fusion | flops 2519728128 | bytes 20057088 | tf_op jit(solution)/shard_map/dot_general | solution.py:140
  300.9 1.6 copy-done.48
  302.6 4.4 fusion.138
  307.2 424.0 %all-gather.3.cloned.1.call-done = f32[8192,768]{1,0:T(8,128)} async-done(((f32[2048,768]{1,0:T(8,128)}), f32[8192,768]{1,0:T(8,128)}) %all-gather.3.cloned.1.call-update) | async-done | bytes 25165840 | tf_op jit(solution)/shard_map/all_gather | solution.py:145
  731.2 12.6 reduce_sum.191
  743.8 5.7 fusion.128
  751.3 4.0 fusion.97
  755.4 5.3 fusion.126
  760.7 9.0 convert_reduce_fusion.1
  769.7 1.6 copy-done.47
  771.3 4.5 fusion.139
  778.2 218.8 %all-reduce.7.cloned.1.call-done = f32[2048,768]{1,0:T(8,128)} async-done(((f32[2048,768]{1,0:T(8,128)}), f32[2048,768]{1,0:T(8,128)}) %all-reduce.7.cloned.1.call-update) | async-done | bytes 6291472 | tf_op jit(solution)/shard_map/psum | solution.py:175
  997.0 8.1 multiply_reduce_fusion.2
  1005.2 4.7 fusion.125
  1009.9 2.6 copy-done.3
  1014.8 1.4 reshape.231
  1016.3 22.0 %while.55 = (s32[]{:T(128)}, bf16[3,512,3,64]{1,3,2,0:T(8,128)(2,1)}, bf16[3,512,3,64]{1,3,2,0:T(8,128)(2,1)}, bf16[3,512,3,64]{1,3,2,0:T(8,128)(2,1)}, bf16[3,5...) while((s32[]{:T(128)}, ...), condition=%wide.region_24.25_spmd, body=%wide.region_22.24_spmd.sunk | while | flops 510589952 | bytes 40343856 | solution.py:197
  1016.3 1.6 fusion.221
  1023.7 1.5 fusion.221
  1031.0 1.5 fusion.221
  1039.5 5.0 fusion.119
  1045.0 9.6 while.54
  1054.6 1.8 copy.118
  1056.4 1.5 stack.63
  1057.9 1.6 copy.117
  1059.5 1.6 stack.62
  1061.0 1.6 copy.116
  1062.6 1.5 stack.61
  1065.4 1.2 copy.110
  1068.8 4.9 fusion.116
  1073.8 4.4 copy.129
  1078.2 4.7 reshape.243
  1083.0 4.8 convolution_bitcast_fusion.1
  1087.8 7.0 fusion.140
  1095.2 7.9 fusion.110
  1104.4 2.1 slice.146
  1106.4 3.2 slice.147
  1109.6 1.4 copy.140
  1113.4 13.3 all-reduce
  1130.4 14.8 reduce-scatter.25.cloned.1.call-done
  1145.2 1.6 copy.134
  1146.8 42.0 %reduce-scatter.23.cloned.1.call-done = f32[96,576]{1,0:T(8,128)} async-done(((f32[768,576]{1,0:T(8,128)}), f32[96,576]{1,0:T(8,128)}) %reduce-scatter.23.cloned.1.call-update) | async-done | bytes 221200
  1190.7 223.4 %all-reduce.9.cloned.1.call-done = f32[2048,768]{1,0:T(8,128)} async-done(((f32[2048,768]{1,0:T(8,128)}), f32[2048,768]{1,0:T(8,128)}) %all-reduce.9.cloned.1.call-update) | async-done | bytes 6291472 | tf_op jit(solution)/shard_map/psum | solution.py:226
  1414.0 5.5 add.173
  1419.5 1.2 slice.150
  1420.8 2.5 slice.151
  1423.3 35.8 %reduce-scatter.19.cloned.1.call-done = f32[96,768]{1,0:T(8,128)} async-done(((f32[768,768]{1,0:T(8,128)}), f32[96,768]{1,0:T(8,128)}) %reduce-scatter.19.cloned.1.call-update) | async-done | bytes 294928 | tf_op jit(solution)/shard_map/reduce_scatter | solution.py:170
  1459.1 46.3 %reduce-scatter.21.cloned.1.call-done = f32[768,96]{0,1:T(8,128)} async-done(((f32[768,768]{0,1:T(8,128)}), f32[768,96]{0,1:T(8,128)}) %reduce-scatter.21.cloned.1.call-update) | async-done | bytes 294928 | tf_op jit(solution)/shard_map/reduce_scatter | solution.py:171
  (307 shorter events, 66.2 us)
Async XLA Ops:
  7.2 275.3 %copy-start = (bf16[768,768]{1,0:T(8,128)(2,1)S(1)}, bf16[768,768]{1,0:T(8,128)(2,1)}, u32[]{:S(2)}) copy-start(bf16[768,768]{1,0:T(8,128)(2,1)} %param.33) | copy-start | bytes 3538948
  7.2 268.4 %all-reduce.5.cloned.1.call-start = ((), (), s32[]{:S(2)}) async-start(), calls=%async_computation.7 | async-start | bytes 12582912 | tf_op jit(solution)/shard_map/psum | solution.py:136
  12.5 1.9 copy-start.44
  18.5 3.0 copy-start.5
  18.5 3.0 copy-start.7
  18.5 9.8 copy-start.43
  28.3 17.8 %copy-start.21 = (bf16[192,768]{1,0:T(8,128)(2,1)S(1)}, bf16[192,768]{1,0:T(8,128)(2,1)}, u32[]{:S(2)}) copy-start(bf16[192,768]{1,0:T(8,128)(2,1)} %param.29) | copy-start | bytes 884740
  46.1 3.8 copy-start.10
  46.1 4.4 copy-start.37
  46.1 4.4 copy-start.38
  46.1 4.4 copy-start.39
  46.2 4.4 copy-start.36
  49.9 681.3 %all-gather.3.cloned.1.call-start = ((), (), s32[]{:S(2)}) async-start(), calls=%async_computation.12 | async-start | bytes 31457280 | tf_op jit(solution)/shard_map/all_gather | solution.py:145
  279.8 2.7 copy-start.2
  282.5 18.4 %copy-start.14 = (bf16[2048,768]{1,0:T(8,128)(2,1)}, bf16[2048,768]{1,0:T(8,128)(2,1)S(1)}, u32[]{:S(2)}) copy-start(bf16[2048,768]{1,0:T(8,128)(2,1)S(1)} %fusion.103) | copy-start | bytes 9437188
  282.5 20.0 %copy-start.40 = (bf16[768,768]{1,0:T(8,128)(2,1)S(1)}, bf16[768,768]{1,0:T(8,128)(2,1)}, u32[]{:S(2)}) copy-start(bf16[768,768]{1,0:T(8,128)(2,1)} %param.35) | copy-start | bytes 3538948
  300.9 1.6 copy-start.48
  307.0 690.0 %all-reduce.7.cloned.1.call-start = ((), (), s32[]{:S(2)}) async-start(), calls=%async_computation.8 | async-start | bytes 12582912 | tf_op jit(solution)/shard_map/psum | solution.py:175
  749.5 1.7 copy-start.9
  749.5 1.8 copy-start.12
  751.3 9.3 slice-start.1
  755.4 5.3 copy-start.41
  755.4 5.3 slice-start.2
  760.6 9.0 copy-start.4
  769.7 1.6 copy-start.47
  775.9 333.8 %reduce-scatter.31.cloned.1.call-start = ((), (), s32[]{:S(2)}) async-start(), calls=%async_computation.17 | async-start | bytes 442368
  776.9 334.1 %reduce-scatter.29.cloned.1.call-start = ((), (), s32[]{:S(2)}) async-start(), calls=%async_computation.16 | async-start | bytes 442368
  778.0 349.4 %reduce-scatter.27.cloned.1.call-start = ((), (), s32[]{:S(2)}) async-start(), calls=%async_computation.15 | async-start | bytes 442368
  1009.9 2.7 copy-start.3
  1016.3 23.2 %copy-start.11 = (bf16[2048,192]{0,1:T(8,128)(2,1)S(1)}, bf16[2048,192]{0,1:T(8,128)(2,1)}, u32[]{:S(2)}) copy-start(bf16[2048,192]{0,1:T(8,128)(2,1)} %copy-done.10) | copy-start | bytes 2359300
  1019.2 2.0 copy-start.28
  1020.4 1.3 copy-start.30
  1020.4 1.9 copy-start.32
  1026.5 2.0 copy-start.28
  1027.7 1.3 copy-start.30
  1027.7 1.9 copy-start.32
  1028.9 1.3 copy-start.29
  1033.8 2.0 copy-start.28
  1035.0 1.3 copy-start.30
  1035.0 1.9 copy-start.32
  1036.3 1.3 copy-start.29
  1038.3 6.2 slice-start
  1038.3 6.6 copy-start.6
  1038.3 6.6 copy-start.8
  1038.3 6.6 copy-start.16
  1038.4 6.6 copy-start.35
  1038.4 6.6 copy-start.45
  1039.4 105.7 %reduce-scatter.25.cloned.1.call-start = ((), (), s32[]{:S(2)}) async-start(), calls=%async_computation.14 | async-start | bytes 884736
  1044.7 144.1 %reduce-scatter.23.cloned.1.call-start = ((), (), s32[]{:S(2)}) async-start(), calls=%async_computation.13 | async-start | bytes 2211840
  1054.6 14.2 copy-start.17
  1065.4 2.7 copy-start.22
  1066.8 1.4 copy-start.24
  1073.7 9.2 copy-start.18
  1073.7 9.2 copy-start.19
  1073.7 9.2 copy-start.20
  1073.7 9.2 copy-start.23
  1073.7 9.2 copy-start.25
  1073.7 9.2 copy-start.27
  1073.8 9.2 copy-start.42
  1082.9 331.2 %all-reduce.9.cloned.1.call-start = ((), (), s32[]{:S(2)}) async-start(), calls=%async_computation.9 | async-start | bytes 12582912 | tf_op jit(solution)/shard_map/psum | solution.py:226
  1087.8 371.3 %reduce-scatter.19.cloned.1.call-start = ((), (), s32[]{:S(2)}) async-start(), calls=%async_computation.10 | async-start | bytes 2654208 | tf_op jit(solution)/shard_map/reduce_scatter | solution.py:170
  1094.9 8.3 copy-start.46
  1094.9 410.5 %reduce-scatter.21.cloned.1.call-start = ((), (), s32[]{:S(2)}) async-start(), calls=%async_computation.11 | async-start | bytes 2654208 | tf_op jit(solution)/shard_map/reduce_scatter | solution.py:171
  1414.0 91.4 %copy-start.1 = (bf16[768,768]{1,0:T(8,128)(2,1)S(1)}, bf16[768,768]{1,0:T(8,128)(2,1)}, u32[]{:S(2)}) copy-start(bf16[768,768]{1,0:T(8,128)(2,1)} %param.33) | copy-start | bytes 3538948
  (11 other events, 9.3 us)
Sparse Core Ops, SparseCore 0:
  50.0 225.5 all-reduce.4
  307.1 424.0 all-gather.2
  776.0 221.0 all-reduce.6
  999.9 32.7 reduce-scatter.30
  1035.7 33.9 reduce-scatter.28
  1072.6 33.8 reduce-scatter.26
  1110.2 34.9 reduce-scatter.24
  1148.6 40.1 reduce-scatter.22
  1191.2 222.8 all-reduce.8
  1417.8 41.2 reduce-scatter.18
  1463.0 42.3 reduce-scatter.20
